TPU v7x, 256 devices: a whole 4x4x8 slice. The times are simulated.
256 devices in a mesh: view: 16 (over z, core), blk: 16 (over y, x).
Axes of the slice: x: 4, y: 4, z: 8, core: 2. Of those that a mesh axis runs over, the one named last changes fastest.
Arguments:
- estimate: float32 [256, 128, 128], P('blk'), may hold values from 0.5 to 2
- images: bfloat16 [16, 256, 64, 128], P('view', 'blk'), may hold values from 0.5 to 2
- point_spread: float32 [8, 9, 7, 25], replicated, may hold values from 0.01 to 1
- covered: int32 [8, 16, 4], P(None, 'blk'), may hold values from 0 to 1, as said below
Outputs:
- estimate_next: float32 [256, 128, 128], P('blk')
Inputs may be any that keep to these rules, and one draw needn't show every extreme that they name: For each view and each block layer along the first dimension, the covered blocks are consecutive along the second dimension and at most 3; for every view some block layer has exactly 3.
All inputs are finite; a program needn't handle non-finite values.
Results may differ from a plain program's by a relative error of at most 0.0003.
Values may be sent and summed in bfloat16 or wider, within the bound.
A program may use at most 64 MiB of HBM per device.

v0:
```python
import jax
import jax.numpy as jnp
from jax import lax
from jax.sharding import PartitionSpec as P

BY = 32


def with_halo(cells, sides, width):
    for axis, dim in sides:
        count = lax.axis_size(axis)
        ends = count - 1
        head = lax.slice_in_dim(cells, 0, width, axis=dim)
        tail = lax.slice_in_dim(cells, cells.shape[dim] - width, cells.shape[dim], axis=dim)
        cells = jnp.concatenate(
            [
                lax.ppermute(tail, axis, [(i, (i + 1) % count) for i in range(ends)]),
                cells,
                lax.ppermute(head, axis, [((i + 1) % count, i) for i in range(ends)]),
            ],
            axis=dim,
        )
    return cells


def swapped(block, axis, stride):
    count = lax.axis_size(axis)
    route = []
    for low in range(count):
        high = low | 1 << stride
        if high != low and high < count:
            route += [(low, high), (high, low)]
    return lax.ppermute(block, axis, route)


def merged(part, axis, combine):
    gathered = lax.all_gather(part, axis)

    def take(source):
        return lax.dynamic_index_in_dim(gathered, source, 0, False)

    return lax.fori_loop(
        1, lax.axis_size(axis), lambda source, state: combine(state, take(source)), take(0)
    )


def band_table(kernel, depth):
    taps_x, taps_y, taps_z = kernel.shape
    span_z = depth + taps_z - 1
    shape_three = (taps_z, span_z, depth)
    offset = lax.broadcasted_iota(jnp.int32, shape_three, 1) - lax.broadcasted_iota(
        jnp.int32, shape_three, 2
    )
    onehot = (offset == lax.broadcasted_iota(jnp.int32, shape_three, 0)).astype(jnp.bfloat16)
    banded = jnp.einsum("abt,tpz->abpz", kernel, onehot, preferred_element_type=jnp.float32).astype(
        jnp.bfloat16
    )
    inner_width = taps_y * span_z
    padded_width = -(-inner_width // 128) * 128
    banded = banded.reshape(taps_x, inner_width, depth)
    return jnp.pad(banded, ((0, 0), (0, padded_width - inner_width), (0, 0)))


def convolve(padded_part, banded, rows_x, rows_y):
    taps_x = padded_part.shape[0] - rows_x + 1
    taps_y = padded_part.shape[1] - rows_y + 1
    columns = jnp.concatenate(
        [padded_part[:, step_y : step_y + rows_y, :] for step_y in range(taps_y)], axis=2
    )
    columns = jnp.pad(columns, ((0, 0), (0, 0), (0, banded.shape[1] - columns.shape[2])))
    output = None
    for shift_x in range(taps_x):
        partial_sum = jnp.dot(
            columns[shift_x : shift_x + rows_x].reshape(rows_x * rows_y, -1),
            banded[shift_x],
            preferred_element_type=jnp.float32,
        )
        output = partial_sum if output is None else output + partial_sum
    return output.reshape(rows_x, rows_y, -1)


def local(estimate, images, point_spread, covered):
    slab_x, width_y, depth = estimate.shape
    share_w = images.shape[2]
    view_count, taps_x, taps_y, taps_z = point_spread.shape
    rim_x, rim_y, rim_z = ((taps_x - 1) // 2, (taps_y - 1) // 2, (taps_z - 1) // 2)
    shares = width_y // share_w
    share_blocks = share_w // BY
    group = lax.axis_index("view")
    view_id = group // shares
    part = group % shares
    y_start = part * share_w
    source = estimate.astype(jnp.bfloat16)
    rimmed = with_halo(source, (("blk", 0),), rim_x)
    padded = jnp.pad(rimmed, ((0, 0), (rim_y, rim_y), (rim_z, rim_z)))
    spread = lax.dynamic_index_in_dim(point_spread, view_id, 0, keepdims=False)
    kernel = (spread / jnp.sum(spread)).astype(jnp.bfloat16)
    forward = band_table(kernel, depth)
    backward = band_table(kernel[::-1, ::-1, ::-1], depth)
    coverage_row = lax.dynamic_index_in_dim(covered[:, 0, :], view_id, 0, keepdims=False) > 0
    share_cover = lax.dynamic_slice_in_dim(coverage_row, part * share_blocks, share_blocks)
    cell_cover = jnp.repeat(share_cover, BY)[None, :, None]
    image = images[0]
    region = lax.dynamic_slice(
        padded, (0, y_start, 0), (slab_x + 2 * rim_x, share_w + 2 * rim_y, depth + 2 * rim_z)
    )
    blurred = convolve(region, forward, slab_x, share_w)
    quotient = jnp.where(cell_cover, image.astype(jnp.float32) / blurred, 0.0).astype(jnp.bfloat16)
    rim_zeros = jnp.zeros((slab_x, rim_y, depth), jnp.bfloat16)
    edge_rows = jnp.where(part == 0, quotient[:, share_w - rim_y :, :], quotient[:, :rim_y, :])
    partner = swapped(edge_rows, "view", 0)
    lower_rim = jnp.where(part > 0, partner, rim_zeros)
    upper_rim = jnp.where(part < shares - 1, partner, rim_zeros)
    extended = jnp.concatenate([lower_rim, quotient, upper_rim], axis=1)
    quotient_rimmed = with_halo(extended, (("blk", 0),), rim_x)
    padded_quotient = jnp.pad(quotient_rimmed, ((0, 0), (0, 0), (rim_z, rim_z)))
    correction = convolve(padded_quotient, backward, slab_x, share_w)
    share_factor = jnp.where(cell_cover, correction, 1.0)
    n_view = lax.axis_size("view")
    step_x = slab_x // n_view
    rows = share_factor.reshape(n_view, step_x, share_w, depth)
    got = lax.all_to_all(rows, "view", 0, 0)
    got = got.reshape(n_view // shares, shares, step_x, share_w, depth)
    product_rows = jnp.prod(got, axis=0)
    product_rows = jnp.transpose(product_rows, (1, 0, 2, 3)).reshape(step_x, width_y, depth)
    mine = lax.dynamic_slice_in_dim(estimate, group * step_x, step_x, axis=0)
    return lax.all_gather(mine * product_rows, "view", axis=0, tiled=True)


def solution(mesh):
    in_specs = (P("blk", None, None), P("view", "blk", None, None), P(), P(None, "blk", None))
    out_specs = P("blk", None, None)
    return jax.shard_map(local, mesh=mesh, in_specs=in_specs, out_specs=out_specs, check_vma=False)
```

profile of v0, /device:TPU:1, one launch (start us, length us, event | category | flops | bytes accessed | tf_op | source)
XLA Modules:
  0.0 175.8 jit_solution(12433264027804252495)
XLA Ops:
  6.5 1.3 convert_element_type.38
  7.9 4.0 %collective-permute-start = (bf16[4,128,128]{2,1,0:T(8,128)(2,1)S(1)}, bf16[4,128,128]{2,1,0:T(8,128)(2,1)S(1)}, u32[]{:S(2)}, u32[]{:S(2)}) collective-permute-start(bf16[4,128,128]{2,1,0:T(8,128)(2,1)S(1)} %get-tuple-element.40), channel_id=1, source_target_pairs={{0,1},{1,2},{2,3},{3,4},{4,5},{5,6},{6,7},{7,8},{8,9},{9,10},{10,1... | collective-permute-start | bytes 393224 | tf_op jit(solution)/shard_map/ppermute | solution.py:17
  11.8 1.3 collective-permute-start.1
  13.2 1.7 fusion.97
  14.8 3.2 %fusion.10 = bf16[9,7,152,128]{3,1,2,0:T(8,128)(2,1)} fusion(f32[1,9,7,25]{3,0,2,1:T(1,128)S(1)} %get-tuple-element.6, f32[]{:T(128)} %get-tuple-element.5), kind=kOutput, calls=%fused_computation.13 | convolution fusion | flops 63488080 | bytes 2457760 | tf_op jit(solution)/shard_map/abt,tpz->abpz/dot_general | solution.py:55
  18.0 1.6 iota_compare_fusion
  19.6 2.1 %copy.10 = bf16[9,7,152,128]{3,2,1,0:T(8,128)(2,1)S(1)} copy(bf16[9,7,152,128]{3,1,2,0:T(8,128)(2,1)} %fusion.10) | data formatting | bytes 4902912 | tf_op jit(solution)/shard_map/convert_element_type | solution.py:55
  22.1 2.9 %fusion.23 = bf16[24,70,152]{2,1,0:T(8,128)(2,1)S(1)} fusion(s32[]{:T(128)S(6)} %select_n.67, bf16[4,128,128]{2,1,0:T(8,128)(2,1)S(1)} %collective-permute-done, bf16[16,128,128]{2,1,0:T(8,128)(2,1)S(1)} %convert_element_type.38, pred[24,134,152]{2,1,0:T(8,128)(4,1)} %get-tuple-element.45, pred[24,134,152]{2,1,0:T(8,128)(4,1)} %get-tuple-element.46, ...), kind=kLoop, calls=%fused_computation.61 | loop fusion | flops 5873280 | bytes 1808896 | tf_op jit(solution)/shard_map/concatenate | solution.py:15
  25.0 3.1 %fusion.99 = (bf16[24,64,152]{2,1,0:T(8,128)(2,1)S(1)}, bf16[24,64,152]{2,1,0:T(8,128)(2,1)}, bf16[24,64,152]{2,1,0:T(8,128)(2,1)}, bf16[24,64,152]{2,1,0:T(8,12...) fusion(bf16[24,70,152]{2,1,0:T(8,128)(2,1)S(1)} %fusion.23), kind=kLoop, calls=%fused_computation.152 | loop fusion | bytes 6537216 | tf_op jit(solution)/shard_map/slice | solution.py:68
  28.1 8.4 %concatenate.16 = bf16[24,64,1064]{2,1,0:T(8,128)(2,1)} concatenate(bf16[24,64,152]{2,1,0:T(8,128)(2,1)} %get-tuple-element.38, bf16[24,64,152]{2,1,0:T(8,128)(2,1)} %get-tuple-element.37, bf16[24,64,152]{2,1,0:T(8,128)(2,1)} %get-tuple-element.36, bf16[24,64,152]{2,1,0:T(8,128)(2,1)} %get-tuple-element.35, bf16[24,64,152]{2,1,0:T(8,128)(2,1)} %get-tuple-element.34, ...), dimensions={2} | concatenate | bytes 6537216 | tf_op jit(solution)/shard_map/concatenate | solution.py:67
  36.5 12.6 %pad_slice_fusion.27 = (bf16[16,64,1152]{2,1,0:T(8,128)(2,1)S(1)}, bf16[16,64,1152]{2,1,0:T(8,128)(2,1)S(1)}, bf16[16,64,1152]{2,1,0:T(8,128)(2,1)S(1)}, bf16[16...) fusion(bf16[24,64,1064]{2,1,0:T(8,128)(2,1)} %concatenate.16), kind=kLoop, calls=%fused_computation.106 | loop fusion | bytes 24502272 | tf_op jit(solution)/shard_map/slice | solution.py:74
  56.6 1.1 collective-permute-start.2
  58.6 1.3 collective-permute-start.4
  59.9 4.9 %collective-permute-start.3 = (bf16[4,70,128]{2,1,0:T(8,128)(2,1)S(1)}, bf16[4,70,128]{2,1,0:T(8,128)(2,1)S(1)}, u32[]{:S(2)}, u32[]{:S(2)}) collective-permute-start(bf16[4,70,128]{2,1,0:T(8,128)(2,1)S(1)} %get-tuple-element.41), channel_id=1, source_target_pairs={{0,1},{1,2},{2,3},{3,4},{4,5},{5,6},{6,7},{7,8},{8,9},{9,10},{10,1... | collective-permute-start | bytes 215048 | tf_op jit(solution)/shard_map/ppermute | solution.py:17
  64.8 1.0 fusion.13
  66.8 3.1 %fusion.98 = (bf16[24,64,152]{2,1,0:T(8,128)(2,1)S(1)}, bf16[24,64,152]{2,1,0:T(8,128)(2,1)}, bf16[24,64,152]{2,1,0:T(8,128)(2,1)}, bf16[24,64,152]{2,1,0:T(8,12...) fusion(bf16[24,70,152]{2,1,0:T(8,128)(2,1)S(1)} %select_maximum_fusion), kind=kLoop, calls=%fused_computation.151 | loop fusion | bytes 6537216 | tf_op jit(solution)/shard_map/slice | solution.py:68
  70.0 8.4 %concatenate.19 = bf16[24,64,1064]{2,1,0:T(8,128)(2,1)} concatenate(bf16[24,64,152]{2,1,0:T(8,128)(2,1)} %get-tuple-element.31, bf16[24,64,152]{2,1,0:T(8,128)(2,1)} %get-tuple-element.30, bf16[24,64,152]{2,1,0:T(8,128)(2,1)} %get-tuple-element.29, bf16[24,64,152]{2,1,0:T(8,128)(2,1)} %get-tuple-element.28, bf16[24,64,152]{2,1,0:T(8,128)(2,1)} %get-tuple-element.27, ...), dimensions={2} | concatenate | bytes 6537216 | tf_op jit(solution)/shard_map/concatenate | solution.py:67
  78.4 12.6 %pad_slice_fusion.18 = (bf16[16,64,1152]{2,1,0:T(8,128)(2,1)S(1)}, bf16[16,64,1152]{2,1,0:T(8,128)(2,1)S(1)}, bf16[16,64,1152]{2,1,0:T(8,128)(2,1)S(1)}, bf16[16...) fusion(bf16[24,64,1064]{2,1,0:T(8,128)(2,1)} %concatenate.19), kind=kLoop, calls=%fused_computation.97 | loop fusion | bytes 24502272 | tf_op jit(solution)/shard_map/slice | solution.py:74
  98.1 0.9 broadcast_select_fusion
  99.0 9.7 %all-to-all-start = ((f32[16,1,64,128]{3,2,1,0:T(8,128)}), f32[16,1,64,128]{3,2,1,0:T(8,128)S(1)}, u32[]{:S(2)}, u32[]{:S(2)}) async-start(f32[16,1,64,128]{3,2,1,0:T(8,128)} %broadcast_select_fusion), calls=%async_computation | async-start | bytes 1048576 | tf_op jit(solution)/shard_map/all_to_all | solution.py:122
  108.7 17.3 %all-to-all-done = f32[16,1,64,128]{3,2,1,0:T(8,128)S(1)} async-done(((f32[16,1,64,128]{3,2,1,0:T(8,128)}), f32[16,1,64,128]{3,2,1,0:T(8,128)S(1)}, u32[]{:S(2)}, u32[]{:S(2)}) %all-to-all-start) | async-done | bytes 524320 | tf_op jit(solution)/shard_map/all_to_all | solution.py:122
  126.0 1.5 bitcast_multiply_fusion
  127.5 39.1 %all-gather.2.cloned.1.call-done = f32[16,128,128]{2,1,0:T(8,128)} async-done(((f32[1,128,128]{2,1,0:T(8,128)}), f32[16,128,128]{2,1,0:T(8,128)}) %all-gather.2.cloned.1.call-update) | async-done | bytes 1048592 | tf_op jit(solution)/shard_map/all_gather | solution.py:127
  166.7 2.3 %copy.26 = f32[16,128,128]{2,1,0:T(8,128)} copy(f32[16,128,128]{2,1,0:T(8,128)} %all-gather.2.cloned.1.call-done) | data formatting | bytes 2097152
  (43 shorter events, 16.8 us)
Async XLA Ops:
  7.9 14.2 %collective-permute-start = (bf16[4,128,128]{2,1,0:T(8,128)(2,1)S(1)}, bf16[4,128,128]{2,1,0:T(8,128)(2,1)S(1)}, u32[]{:S(2)}, u32[]{:S(2)}) collective-permute-start(bf16[4,128,128]{2,1,0:T(8,128)(2,1)S(1)} %get-tuple-element.40), channel_id=1, source_target_pairs={{0,1},{1,2},{2,3},{3,4},{4,5},{5,6},{6,7},{7,8},{8,9},{9,10},{10,1... | collective-permute-start | bytes 393224 | tf_op jit(solution)/shard_map/ppermute | solution.py:17
  11.8 10.3 %collective-permute-start.1 = (bf16[4,128,128]{2,1,0:T(8,128)(2,1)S(1)}, bf16[4,128,128]{2,1,0:T(8,128)(2,1)S(1)}, u32[]{:S(2)}, u32[]{:S(2)}) collective-permute-start(bf16[4,128,128]{2,1,0:T(8,128)(2,1)S(1)} %get-tuple-element.39), channel_id=1, source_target_pairs={{1,0},{2,1},{3,2},{4,3},{5,4},{6,5},{7,6},{8,7},{9,8},{10,9},{11,1... | collective-permute-start | bytes 393224 | tf_op jit(solution)/shard_map/ppermute | solution.py:19
  19.6 2.2 %copy-start.1 = (s32[8,1,4]{0,2,1:T(4,128)S(1)}, s32[8,1,4]{0,2,1:T(4,128)}, u32[]{:S(2)}) copy-start(s32[8,1,4]{0,2,1:T(4,128)} %param.7) | copy-start | bytes 388
  55.4 1.0 copy-start
  56.6 1.9 %collective-permute-start.2 = (bf16[16,3,128]{2,1,0:T(4,128)(2,1)S(1)}, bf16[16,3,128]{2,1,0:T(4,128)(2,1)S(1)}, u32[]{:S(2)}, u32[]{:S(2)}) collective-permute-start(bf16[16,3,128]{2,1,0:T(4,128)(2,1)S(1)} %slice_select_fusion), channel_id=1, source_target_pairs={{0,16},{16,0},{32,48},{48,32},{64,80},{80,64},{96,112},{112,96},{1... | collective-permute-start | bytes 36872 | tf_op jit(solution)/shard_map/ppermute | solution.py:33
  58.6 7.5 %collective-permute-start.4 = (bf16[4,70,128]{2,1,0:T(8,128)(2,1)S(1)}, bf16[4,70,128]{2,1,0:T(8,128)(2,1)S(1)}, u32[]{:S(2)}, u32[]{:S(2)}) collective-permute-start(bf16[4,70,128]{2,1,0:T(8,128)(2,1)S(1)} %get-tuple-element.42), channel_id=1, source_target_pairs={{1,0},{2,1},{3,2},{4,3},{5,4},{6,5},{7,6},{8,7},{9,8},{10,9},{11,1... | collective-permute-start | bytes 215048 | tf_op jit(solution)/shard_map/ppermute | solution.py:19
  59.9 6.3 %collective-permute-start.3 = (bf16[4,70,128]{2,1,0:T(8,128)(2,1)S(1)}, bf16[4,70,128]{2,1,0:T(8,128)(2,1)S(1)}, u32[]{:S(2)}, u32[]{:S(2)}) collective-permute-start(bf16[4,70,128]{2,1,0:T(8,128)(2,1)S(1)} %get-tuple-element.41), channel_id=1, source_target_pairs={{0,1},{1,2},{2,3},{3,4},{4,5},{5,6},{6,7},{7,8},{8,9},{9,10},{10,1... | collective-permute-start | bytes 215048 | tf_op jit(solution)/shard_map/ppermute | solution.py:17
  99.0 27.0 %all-to-all-start = ((f32[16,1,64,128]{3,2,1,0:T(8,128)}), f32[16,1,64,128]{3,2,1,0:T(8,128)S(1)}, u32[]{:S(2)}, u32[]{:S(2)}) async-start(f32[16,1,64,128]{3,2,1,0:T(8,128)} %broadcast_select_fusion), calls=%async_computation | async-start | bytes 1048576 | tf_op jit(solution)/shard_map/all_to_all | solution.py:122
  108.7 58.0 %all-gather.2.cloned.1.call-start = ((), (), s32[]{:S(2)}) async-start(), calls=%async_computation.1 | async-start | bytes 1114112 | tf_op jit(solution)/shard_map/all_gather | solution.py:127
Sparse Core Ops, SparseCore 0:
  127.7 38.9 all-gather.1
where the time goes:
time: 177 us; the launch traced here: 176 us
  waiting for transfers between devices  56.6 us (32%)
  local copies, waits for them, and re-layouts  53.6 us (30%)
  starting transfers between devices  22.2 us (13%)
  matrix products  18.2 us (10%)
  between operations  13.7 us (8%)
  other arithmetic  11.5 us (6%)
    all_gather x1, waiting for transfers between devices, local(): return lax.all_gather(mine * product_rows, 'view', axis=0, tiled=True)  39.1 us
    slice x2, local copies, waits for them, and re-layouts, convolve(): columns[shift_x:shift_x + rows_x].reshape(rows_x * rows_y, -1)  25.2 us
    all_to_all x1, waiting for transfers between devices, local(): got = lax.all_to_all(rows, 'view', 0, 0)  17.3 us
    concatenate x2, local copies, waits for them, and re-layouts, convolve(): jnp.concatenate([padded_part[:, step_y:step_y + rows_y, :] for step_y in...  16.9 us
    dot_general x18, matrix products, convolve(): jnp.dot(columns[shift_x:shift_x + rows_x].reshape(rows_x * rows_y, -1), b...  14 us
    all_to_all x1, starting transfers between devices, local(): got = lax.all_to_all(rows, 'view', 0, 0)  9.68 us
    ppermute x2, starting transfers between devices, with_halo(): lax.ppermute(tail, axis, [(i, (i + 1) % count) for i in range(ends)])  8.85 us
    slice x2, local copies, waits for them, and re-layouts, convolve(): padded_part[:, step_y:step_y + rows_y, :]  6.25 us
  transfers between devices with their start and end apart: 7, of which 4 were waited for; matrix products, arithmetic and copies ran while one was open for 6% of the time, Pallas kernels for 0%

commit v1 on v0

--- a/solution.py
+++ b/solution.py
@@ -4,6 +4,27 @@
 from jax.sharding import PartitionSpec as P
 
 BY = 32
+
+
+def collect(x, axis, dim):
+    size, here, extent = (lax.axis_size(axis), lax.axis_index(axis), x.shape[dim])
+    ahead = [(i, (i + 1) % size) for i in range(size)]
+    backward = [(i, (i - 1) % size) for i in range(size)]
+    out = jnp.zeros((*x.shape[:dim], size * extent, *x.shape[dim + 1 :]), x.dtype)
+    out = lax.dynamic_update_slice_in_dim(out, x, here * extent, axis=dim)
+    from_left = from_right = x
+    half = size // 2
+    for step in range(1, half + 1):
+        from_left = lax.ppermute(from_left, axis, ahead)
+        out = lax.dynamic_update_slice_in_dim(
+            out, from_left, (here - step) % size * extent, axis=dim
+        )
+        if step < size - half:
+            from_right = lax.ppermute(from_right, axis, backward)
+            out = lax.dynamic_update_slice_in_dim(
+                out, from_right, (here + step) % size * extent, axis=dim
+            )
+    return out
 
 
 def with_halo(cells, sides, width):
@@ -124,7 +145,7 @@
     product_rows = jnp.prod(got, axis=0)
     product_rows = jnp.transpose(product_rows, (1, 0, 2, 3)).reshape(step_x, width_y, depth)
     mine = lax.dynamic_slice_in_dim(estimate, group * step_x, step_x, axis=0)
-    return lax.all_gather(mine * product_rows, "view", axis=0, tiled=True)
+    return collect(mine * product_rows, "view", 0)
 
 
 def solution(mesh):

time: 177 us -> 166 us (0.938)
  the two profiles are of different devices: /device:TPU:1 before, /device:TPU:6 now
where the time goes in v1:
time: 166 us; the launch traced here: 164 us
  local copies, waits for them, and re-layouts  52.4 us (32%)
  starting transfers between devices  42.6 us (26%)
  waiting for transfers between devices  39.8 us (24%)
  matrix products  18.2 us (11%)
  other arithmetic  11 us (7%)
    slice x2, local copies, waits for them, and re-layouts, convolve(): columns[shift_x:shift_x + rows_x].reshape(rows_x * rows_y, -1)  25.4 us
    ppermute x7, starting transfers between devices, collect(): from_right = lax.ppermute(from_right, axis, backward)  19 us
    ppermute x8, waiting for transfers between devices, collect(): from_left = lax.ppermute(from_left, axis, ahead)  18.2 us
    concatenate x2, local copies, waits for them, and re-layouts, convolve(): jnp.concatenate([padded_part[:, step_y:step_y + rows_y, :] for step_y in...  16.8 us
    all_to_all x1, waiting for transfers between devices, local(): got = lax.all_to_all(rows, 'view', 0, 0)  16 us
    dot_general x18, matrix products, convolve(): jnp.dot(columns[shift_x:shift_x + rows_x].reshape(rows_x * rows_y, -1), b...  14 us
    ppermute x2, starting transfers between devices, with_halo(): lax.ppermute(tail, axis, [(i, (i + 1) % count) for i in range(ends)])  8.91 us
    all_to_all x1, starting transfers between devices, local(): got = lax.all_to_all(rows, 'view', 0, 0)  8.57 us
  transfers between devices with their start and end apart: 21, of which 11 were waited for; matrix products, arithmetic and copies ran while one was open for 7% of the time, Pallas kernels for 0%

profile of v1, /device:TPU:6, one launch (start us, length us, event | category | flops | bytes accessed | tf_op | source)
XLA Modules:
  0.0 164.4 jit_solution(736800878585628629)
XLA Ops:
  1.3 3.4 %collective-permute-start = (bf16[4,128,128]{2,1,0:T(8,128)(2,1)S(1)}, bf16[4,128,128]{2,1,0:T(8,128)(2,1)S(1)}, u32[]{:S(2)}, u32[]{:S(2)}) collective-permute-start(bf16[4,128,128]{2,1,0:T(8,128)(2,1)S(1)} %get-tuple-element.42), channel_id=1, source_target_pairs={{0,1},{1,2},{2,3},{3,4},{4,5},{5,6},{6,7},{7,8},{8,9},{9,10},{10,1... | collective-permute-start | bytes 393224 | tf_op jit(solution)/shard_map/ppermute | solution.py:38
  4.8 2.4 %collective-permute-start.1 = (bf16[4,128,128]{2,1,0:T(8,128)(2,1)S(1)}, bf16[4,128,128]{2,1,0:T(8,128)(2,1)S(1)}, u32[]{:S(2)}, u32[]{:S(2)}) collective-permute-start(bf16[4,128,128]{2,1,0:T(8,128)(2,1)S(1)} %get-tuple-element.41), channel_id=1, source_target_pairs={{1,0},{2,1},{3,2},{4,3},{5,4},{6,5},{7,6},{8,7},{9,8},{10,9},{11,1... | collective-permute-start | bytes 393224 | tf_op jit(solution)/shard_map/ppermute | solution.py:40
  8.9 3.2 %fusion.10 = bf16[9,7,152,128]{3,1,2,0:T(8,128)(2,1)} fusion(f32[1,9,7,25]{3,0,2,1:T(1,128)S(1)} %get-tuple-element.8, f32[]{:T(128)} %get-tuple-element.7), kind=kOutput, calls=%fused_computation.13 | convolution fusion | flops 63488080 | bytes 2457760 | tf_op jit(solution)/shard_map/abt,tpz->abpz/dot_general | solution.py:76
  13.7 2.1 %copy.10 = bf16[9,7,152,128]{3,2,1,0:T(8,128)(2,1)S(1)} copy(bf16[9,7,152,128]{3,1,2,0:T(8,128)(2,1)} %fusion.10) | data formatting | bytes 4902912 | tf_op jit(solution)/shard_map/convert_element_type | solution.py:76
  16.3 2.9 %fusion.23 = bf16[24,70,152]{2,1,0:T(8,128)(2,1)S(1)} fusion(s32[]{:T(128)S(6)} %select_n.173, bf16[4,128,128]{2,1,0:T(8,128)(2,1)S(1)} %collective-permute-done, bf16[16,128,128]{2,1,0:T(8,128)(2,1)S(1)} %convert_element_type.38, pred[24,134,152]{2,1,0:T(8,128)(4,1)} %get-tuple-element.47, pred[24,134,152]{2,1,0:T(8,128)(4,1)} %get-tuple-element.48, ...), kind=kLoop, calls=%fused_computation.61 | loop fusion | flops 5873280 | bytes 1808896 | tf_op jit(solution)/shard_map/concatenate | solution.py:36
  19.2 3.1 %fusion.99 = (bf16[24,64,152]{2,1,0:T(8,128)(2,1)S(1)}, bf16[24,64,152]{2,1,0:T(8,128)(2,1)}, bf16[24,64,152]{2,1,0:T(8,128)(2,1)}, bf16[24,64,152]{2,1,0:T(8,12...) fusion(bf16[24,70,152]{2,1,0:T(8,128)(2,1)S(1)} %fusion.23), kind=kLoop, calls=%fused_computation.168 | loop fusion | bytes 6537216 | tf_op jit(solution)/shard_map/slice | solution.py:89
  22.3 8.4 %concatenate.16 = bf16[24,64,1064]{2,1,0:T(8,128)(2,1)} concatenate(bf16[24,64,152]{2,1,0:T(8,128)(2,1)} %get-tuple-element.40, bf16[24,64,152]{2,1,0:T(8,128)(2,1)} %get-tuple-element.39, bf16[24,64,152]{2,1,0:T(8,128)(2,1)} %get-tuple-element.38, bf16[24,64,152]{2,1,0:T(8,128)(2,1)} %get-tuple-element.37, bf16[24,64,152]{2,1,0:T(8,128)(2,1)} %get-tuple-element.36, ...), dimensions={2} | concatenate | bytes 6537216 | tf_op jit(solution)/shard_map/concatenate | solution.py:88
  30.7 12.7 %pad_slice_fusion.27 = (bf16[16,64,1152]{2,1,0:T(8,128)(2,1)S(1)}, bf16[16,64,1152]{2,1,0:T(8,128)(2,1)S(1)}, bf16[16,64,1152]{2,1,0:T(8,128)(2,1)S(1)}, bf16[16...) fusion(bf16[24,64,1064]{2,1,0:T(8,128)(2,1)} %concatenate.16), kind=kLoop, calls=%fused_computation.106 | loop fusion | bytes 24502272 | tf_op jit(solution)/shard_map/slice | solution.py:95
  52.2 5.5 %collective-permute-start.3 = (bf16[4,70,128]{2,1,0:T(8,128)(2,1)S(1)}, bf16[4,70,128]{2,1,0:T(8,128)(2,1)S(1)}, u32[]{:S(2)}, u32[]{:S(2)}) collective-permute-start(bf16[4,70,128]{2,1,0:T(8,128)(2,1)S(1)} %get-tuple-element.43), channel_id=1, source_target_pairs={{0,1},{1,2},{2,3},{3,4},{4,5},{5,6},{6,7},{7,8},{8,9},{9,10},{10,1... | collective-permute-start | bytes 215048 | tf_op jit(solution)/shard_map/ppermute | solution.py:38
  57.7 1.9 %collective-permute-start.4 = (bf16[4,70,128]{2,1,0:T(8,128)(2,1)S(1)}, bf16[4,70,128]{2,1,0:T(8,128)(2,1)S(1)}, u32[]{:S(2)}, u32[]{:S(2)}) collective-permute-start(bf16[4,70,128]{2,1,0:T(8,128)(2,1)S(1)} %get-tuple-element.44), channel_id=1, source_target_pairs={{1,0},{2,1},{3,2},{4,3},{5,4},{6,5},{7,6},{8,7},{9,8},{10,9},{11,1... | collective-permute-start | bytes 215048 | tf_op jit(solution)/shard_map/ppermute | solution.py:40
  61.0 5.1 %collective-permute-done.4 = bf16[4,70,128]{2,1,0:T(8,128)(2,1)S(1)} collective-permute-done((bf16[4,70,128]{2,1,0:T(8,128)(2,1)S(1)}, bf16[4,70,128]{2,1,0:T(8,128)(2,1)S(1)}, u32[]{:S(2)}, u32[]{:S(2)}) %collective-permute-start.4) | collective-permute-done | bytes 71712 | tf_op jit(solution)/shard_map/ppermute | solution.py:40
  66.7 3.1 %fusion.98 = (bf16[24,64,152]{2,1,0:T(8,128)(2,1)S(1)}, bf16[24,64,152]{2,1,0:T(8,128)(2,1)}, bf16[24,64,152]{2,1,0:T(8,128)(2,1)}, bf16[24,64,152]{2,1,0:T(8,12...) fusion(bf16[24,70,152]{2,1,0:T(8,128)(2,1)S(1)} %select_maximum_fusion), kind=kLoop, calls=%fused_computation.167 | loop fusion | bytes 6537216 | tf_op jit(solution)/shard_map/slice | solution.py:89
  69.8 8.4 %concatenate.19 = bf16[24,64,1064]{2,1,0:T(8,128)(2,1)} concatenate(bf16[24,64,152]{2,1,0:T(8,128)(2,1)} %get-tuple-element.33, bf16[24,64,152]{2,1,0:T(8,128)(2,1)} %get-tuple-element.32, bf16[24,64,152]{2,1,0:T(8,128)(2,1)} %get-tuple-element.31, bf16[24,64,152]{2,1,0:T(8,128)(2,1)} %get-tuple-element.30, bf16[24,64,152]{2,1,0:T(8,128)(2,1)} %get-tuple-element.29, ...), dimensions={2} | concatenate | bytes 6537216 | tf_op jit(solution)/shard_map/concatenate | solution.py:88
  78.3 12.7 %pad_slice_fusion.18 = (bf16[16,64,1152]{2,1,0:T(8,128)(2,1)S(1)}, bf16[16,64,1152]{2,1,0:T(8,128)(2,1)S(1)}, bf16[16,64,1152]{2,1,0:T(8,128)(2,1)S(1)}, bf16[16...) fusion(bf16[24,64,1064]{2,1,0:T(8,128)(2,1)} %concatenate.19), kind=kLoop, calls=%fused_computation.97 | loop fusion | bytes 24502272 | tf_op jit(solution)/shard_map/slice | solution.py:95
  99.0 8.6 %all-to-all-start = ((f32[16,1,64,128]{3,2,1,0:T(8,128)}), f32[16,1,64,128]{3,2,1,0:T(8,128)S(1)}, u32[]{:S(2)}, u32[]{:S(2)}) async-start(f32[16,1,64,128]{3,2,1,0:T(8,128)} %broadcast_select_fusion), calls=%async_computation | async-start | bytes 1048576 | tf_op jit(solution)/shard_map/all_to_all | solution.py:143
  107.6 16.0 %all-to-all-done = f32[16,1,64,128]{3,2,1,0:T(8,128)S(1)} async-done(((f32[16,1,64,128]{3,2,1,0:T(8,128)}), f32[16,1,64,128]{3,2,1,0:T(8,128)S(1)}, u32[]{:S(2)}, u32[]{:S(2)}) %all-to-all-start) | async-done | bytes 524320 | tf_op jit(solution)/shard_map/all_to_all | solution.py:143
  127.5 1.9 %collective-permute-done.5 = f32[1,128,128]{2,1,0:T(8,128)S(1)} collective-permute-done((f32[1,128,128]{2,1,0:T(8,128)S(1)}, f32[1,128,128]{2,1,0:T(8,128)S(1)}, u32[]{:S(2)}, u32[]{:S(2)}) %collective-permute-start.5) | collective-permute-done | bytes 65568 | tf_op jit(solution)/shard_map/ppermute | solution.py:18
  129.5 3.0 %collective-permute-start.8 = (f32[1,128,128]{2,1,0:T(8,128)S(1)}, f32[1,128,128]{2,1,0:T(8,128)S(1)}, u32[]{:S(2)}, u32[]{:S(2)}) collective-permute-start(f32[1,128,128]{2,1,0:T(8,128)S(1)} %collective-permute-done.6), channel_id=1, source_target_pairs={{0,240},{16,0},{32,16},{48,32},{64,48},{80,64},{96,80},{112,96},{1... | collective-permute-start | bytes 196616 | tf_op jit(solution)/shard_map/ppermute | solution.py:23
  134.4 3.0 %collective-permute-start.10 = (f32[1,128,128]{2,1,0:T(8,128)S(1)}, f32[1,128,128]{2,1,0:T(8,128)S(1)}, u32[]{:S(2)}, u32[]{:S(2)}) collective-permute-start(f32[1,128,128]{2,1,0:T(8,128)S(1)} %collective-permute-done.8), channel_id=1, source_target_pairs={{0,240},{16,0},{32,16},{48,32},{64,48},{80,64},{96,80},{112,96},{1... | collective-permute-start | bytes 196616 | tf_op jit(solution)/shard_map/ppermute | solution.py:23
  139.3 3.0 %collective-permute-start.12 = (f32[1,128,128]{2,1,0:T(8,128)S(1)}, f32[1,128,128]{2,1,0:T(8,128)S(1)}, u32[]{:S(2)}, u32[]{:S(2)}) collective-permute-start(f32[1,128,128]{2,1,0:T(8,128)S(1)} %collective-permute-done.10), channel_id=1, source_target_pairs={{0,240},{16,0},{32,16},{48,32},{64,48},{80,64},{96,80},{112,96},{1... | collective-permute-start | bytes 196616 | tf_op jit(solution)/shard_map/ppermute | solution.py:23
  144.2 3.0 %collective-permute-start.14 = (f32[1,128,128]{2,1,0:T(8,128)S(1)}, f32[1,128,128]{2,1,0:T(8,128)S(1)}, u32[]{:S(2)}, u32[]{:S(2)}) collective-permute-start(f32[1,128,128]{2,1,0:T(8,128)S(1)} %collective-permute-done.12), channel_id=1, source_target_pairs={{0,240},{16,0},{32,16},{48,32},{64,48},{80,64},{96,80},{112,96},{1... | collective-permute-start | bytes 196616 | tf_op jit(solution)/shard_map/ppermute | solution.py:23
  149.1 3.0 %collective-permute-start.16 = (f32[1,128,128]{2,1,0:T(8,128)S(1)}, f32[1,128,128]{2,1,0:T(8,128)S(1)}, u32[]{:S(2)}, u32[]{:S(2)}) collective-permute-start(f32[1,128,128]{2,1,0:T(8,128)S(1)} %collective-permute-done.14), channel_id=1, source_target_pairs={{0,240},{16,0},{32,16},{48,32},{64,48},{80,64},{96,80},{112,96},{1... | collective-permute-start | bytes 196616 | tf_op jit(solution)/shard_map/ppermute | solution.py:23
  154.0 3.0 %collective-permute-start.18 = (f32[1,128,128]{2,1,0:T(8,128)S(1)}, f32[1,128,128]{2,1,0:T(8,128)S(1)}, u32[]{:S(2)}, u32[]{:S(2)}) collective-permute-start(f32[1,128,128]{2,1,0:T(8,128)S(1)} %collective-permute-done.16), channel_id=1, source_target_pairs={{0,240},{16,0},{32,16},{48,32},{64,48},{80,64},{96,80},{112,96},{1... | collective-permute-start | bytes 196616 | tf_op jit(solution)/shard_map/ppermute | solution.py:23
  159.0 4.8 %collective-permute-done.19 = f32[1,128,128]{2,1,0:T(8,128)S(1)} collective-permute-done((f32[1,128,128]{2,1,0:T(8,128)S(1)}, f32[1,128,128]{2,1,0:T(8,128)S(1)}, u32[]{:S(2)}, u32[]{:S(2)}) %collective-permute-start.19) | collective-permute-done | bytes 65568 | tf_op jit(solution)/shard_map/ppermute | solution.py:18
  (87 shorter events, 39.8 us)
Async XLA Ops:
  1.3 14.9 %collective-permute-start = (bf16[4,128,128]{2,1,0:T(8,128)(2,1)S(1)}, bf16[4,128,128]{2,1,0:T(8,128)(2,1)S(1)}, u32[]{:S(2)}, u32[]{:S(2)}) collective-permute-start(bf16[4,128,128]{2,1,0:T(8,128)(2,1)S(1)} %get-tuple-element.42), channel_id=1, source_target_pairs={{0,1},{1,2},{2,3},{3,4},{4,5},{5,6},{6,7},{7,8},{8,9},{9,10},{10,1... | collective-permute-start | bytes 393224 | tf_op jit(solution)/shard_map/ppermute | solution.py:38
  4.8 11.5 %collective-permute-start.1 = (bf16[4,128,128]{2,1,0:T(8,128)(2,1)S(1)}, bf16[4,128,128]{2,1,0:T(8,128)(2,1)S(1)}, u32[]{:S(2)}, u32[]{:S(2)}) collective-permute-start(bf16[4,128,128]{2,1,0:T(8,128)(2,1)S(1)} %get-tuple-element.41), channel_id=1, source_target_pairs={{1,0},{2,1},{3,2},{4,3},{5,4},{6,5},{7,6},{8,7},{9,8},{10,9},{11,1... | collective-permute-start | bytes 393224 | tf_op jit(solution)/shard_map/ppermute | solution.py:40
  13.7 2.2 %copy-start.2 = (s32[8,1,4]{0,2,1:T(4,128)S(1)}, s32[8,1,4]{0,2,1:T(4,128)}, u32[]{:S(2)}) copy-start(s32[8,1,4]{0,2,1:T(4,128)} %param.7) | copy-start | bytes 388
  49.7 1.0 copy-start.1
  50.8 1.3 collective-permute-start.2
  52.2 8.8 %collective-permute-start.3 = (bf16[4,70,128]{2,1,0:T(8,128)(2,1)S(1)}, bf16[4,70,128]{2,1,0:T(8,128)(2,1)S(1)}, u32[]{:S(2)}, u32[]{:S(2)}) collective-permute-start(bf16[4,70,128]{2,1,0:T(8,128)(2,1)S(1)} %get-tuple-element.43), channel_id=1, source_target_pairs={{0,1},{1,2},{2,3},{3,4},{4,5},{5,6},{6,7},{7,8},{8,9},{9,10},{10,1... | collective-permute-start | bytes 215048 | tf_op jit(solution)/shard_map/ppermute | solution.py:38
  57.7 8.4 %collective-permute-start.4 = (bf16[4,70,128]{2,1,0:T(8,128)(2,1)S(1)}, bf16[4,70,128]{2,1,0:T(8,128)(2,1)S(1)}, u32[]{:S(2)}, u32[]{:S(2)}) collective-permute-start(bf16[4,70,128]{2,1,0:T(8,128)(2,1)S(1)} %get-tuple-element.44), channel_id=1, source_target_pairs={{1,0},{2,1},{3,2},{4,3},{5,4},{6,5},{7,6},{8,7},{9,8},{10,9},{11,1... | collective-permute-start | bytes 215048 | tf_op jit(solution)/shard_map/ppermute | solution.py:40
  99.0 24.6 %all-to-all-start = ((f32[16,1,64,128]{3,2,1,0:T(8,128)}), f32[16,1,64,128]{3,2,1,0:T(8,128)S(1)}, u32[]{:S(2)}, u32[]{:S(2)}) async-start(f32[16,1,64,128]{3,2,1,0:T(8,128)} %broadcast_select_fusion), calls=%async_computation | async-start | bytes 1048576 | tf_op jit(solution)/shard_map/all_to_all | solution.py:143
  124.6 4.9 %collective-permute-start.5 = (f32[1,128,128]{2,1,0:T(8,128)S(1)}, f32[1,128,128]{2,1,0:T(8,128)S(1)}, u32[]{:S(2)}, u32[]{:S(2)}) collective-permute-start(f32[1,128,128]{2,1,0:T(8,128)S(1)} %get-tuple-element.6), channel_id=1, source_target_pairs={{0,16},{16,32},{32,48},{48,64},{64,80},{80,96},{96,112},{112,128},... | collective-permute-start | bytes 196616 | tf_op jit(solution)/shard_map/ppermute | solution.py:18
  126.3 3.2 %collective-permute-start.6 = (f32[1,128,128]{2,1,0:T(8,128)S(1)}, f32[1,128,128]{2,1,0:T(8,128)S(1)}, u32[]{:S(2)}, u32[]{:S(2)}) collective-permute-start(f32[1,128,128]{2,1,0:T(8,128)S(1)} %get-tuple-element.6), channel_id=1, source_target_pairs={{0,240},{16,0},{32,16},{48,32},{64,48},{80,64},{96,80},{112,96},{1... | collective-permute-start | bytes 196616 | tf_op jit(solution)/shard_map/ppermute | solution.py:23
  129.5 4.9 %collective-permute-start.7 = (f32[1,128,128]{2,1,0:T(8,128)S(1)}, f32[1,128,128]{2,1,0:T(8,128)S(1)}, u32[]{:S(2)}, u32[]{:S(2)}) collective-permute-start(f32[1,128,128]{2,1,0:T(8,128)S(1)} %collective-permute-done.5), channel_id=1, source_target_pairs={{0,16},{16,32},{32,48},{48,64},{64,80},{80,96},{96,112},{112,128},... | collective-permute-start | bytes 196616 | tf_op jit(solution)/shard_map/ppermute | solution.py:18
  129.5 4.9 %collective-permute-start.8 = (f32[1,128,128]{2,1,0:T(8,128)S(1)}, f32[1,128,128]{2,1,0:T(8,128)S(1)}, u32[]{:S(2)}, u32[]{:S(2)}) collective-permute-start(f32[1,128,128]{2,1,0:T(8,128)S(1)} %collective-permute-done.6), channel_id=1, source_target_pairs={{0,240},{16,0},{32,16},{48,32},{64,48},{80,64},{96,80},{112,96},{1... | collective-permute-start | bytes 196616 | tf_op jit(solution)/shard_map/ppermute | solution.py:23
  134.4 4.9 %collective-permute-start.9 = (f32[1,128,128]{2,1,0:T(8,128)S(1)}, f32[1,128,128]{2,1,0:T(8,128)S(1)}, u32[]{:S(2)}, u32[]{:S(2)}) collective-permute-start(f32[1,128,128]{2,1,0:T(8,128)S(1)} %collective-permute-done.7), channel_id=1, source_target_pairs={{0,16},{16,32},{32,48},{48,64},{64,80},{80,96},{96,112},{112,128},... | collective-permute-start | bytes 196616 | tf_op jit(solution)/shard_map/ppermute | solution.py:18
  134.4 4.9 %collective-permute-start.10 = (f32[1,128,128]{2,1,0:T(8,128)S(1)}, f32[1,128,128]{2,1,0:T(8,128)S(1)}, u32[]{:S(2)}, u32[]{:S(2)}) collective-permute-start(f32[1,128,128]{2,1,0:T(8,128)S(1)} %collective-permute-done.8), channel_id=1, source_target_pairs={{0,240},{16,0},{32,16},{48,32},{64,48},{80,64},{96,80},{112,96},{1... | collective-permute-start | bytes 196616 | tf_op jit(solution)/shard_map/ppermute | solution.py:23
  139.3 4.9 %collective-permute-start.11 = (f32[1,128,128]{2,1,0:T(8,128)S(1)}, f32[1,128,128]{2,1,0:T(8,128)S(1)}, u32[]{:S(2)}, u32[]{:S(2)}) collective-permute-start(f32[1,128,128]{2,1,0:T(8,128)S(1)} %collective-permute-done.9), channel_id=1, source_target_pairs={{0,16},{16,32},{32,48},{48,64},{64,80},{80,96},{96,112},{112,128},... | collective-permute-start | bytes 196616 | tf_op jit(solution)/shard_map/ppermute | solution.py:18
  139.3 4.9 %collective-permute-start.12 = (f32[1,128,128]{2,1,0:T(8,128)S(1)}, f32[1,128,128]{2,1,0:T(8,128)S(1)}, u32[]{:S(2)}, u32[]{:S(2)}) collective-permute-start(f32[1,128,128]{2,1,0:T(8,128)S(1)} %collective-permute-done.10), channel_id=1, source_target_pairs={{0,240},{16,0},{32,16},{48,32},{64,48},{80,64},{96,80},{112,96},{1... | collective-permute-start | bytes 196616 | tf_op jit(solution)/shard_map/ppermute | solution.py:23
  144.2 4.9 %collective-permute-start.13 = (f32[1,128,128]{2,1,0:T(8,128)S(1)}, f32[1,128,128]{2,1,0:T(8,128)S(1)}, u32[]{:S(2)}, u32[]{:S(2)}) collective-permute-start(f32[1,128,128]{2,1,0:T(8,128)S(1)} %collective-permute-done.11), channel_id=1, source_target_pairs={{0,16},{16,32},{32,48},{48,64},{64,80},{80,96},{96,112},{112,128},... | collective-permute-start | bytes 196616 | tf_op jit(solution)/shard_map/ppermute | solution.py:18
  144.2 4.9 %collective-permute-start.14 = (f32[1,128,128]{2,1,0:T(8,128)S(1)}, f32[1,128,128]{2,1,0:T(8,128)S(1)}, u32[]{:S(2)}, u32[]{:S(2)}) collective-permute-start(f32[1,128,128]{2,1,0:T(8,128)S(1)} %collective-permute-done.12), channel_id=1, source_target_pairs={{0,240},{16,0},{32,16},{48,32},{64,48},{80,64},{96,80},{112,96},{1... | collective-permute-start | bytes 196616 | tf_op jit(solution)/shard_map/ppermute | solution.py:23
  149.1 4.9 %collective-permute-start.15 = (f32[1,128,128]{2,1,0:T(8,128)S(1)}, f32[1,128,128]{2,1,0:T(8,128)S(1)}, u32[]{:S(2)}, u32[]{:S(2)}) collective-permute-start(f32[1,128,128]{2,1,0:T(8,128)S(1)} %collective-permute-done.13), channel_id=1, source_target_pairs={{0,16},{16,32},{32,48},{48,64},{64,80},{80,96},{96,112},{112,128},... | collective-permute-start | bytes 196616 | tf_op jit(solution)/shard_map/ppermute | solution.py:18
  149.1 4.9 %collective-permute-start.16 = (f32[1,128,128]{2,1,0:T(8,128)S(1)}, f32[1,128,128]{2,1,0:T(8,128)S(1)}, u32[]{:S(2)}, u32[]{:S(2)}) collective-permute-start(f32[1,128,128]{2,1,0:T(8,128)S(1)} %collective-permute-done.14), channel_id=1, source_target_pairs={{0,240},{16,0},{32,16},{48,32},{64,48},{80,64},{96,80},{112,96},{1... | collective-permute-start | bytes 196616 | tf_op jit(solution)/shard_map/ppermute | solution.py:23
  154.0 4.9 %collective-permute-start.17 = (f32[1,128,128]{2,1,0:T(8,128)S(1)}, f32[1,128,128]{2,1,0:T(8,128)S(1)}, u32[]{:S(2)}, u32[]{:S(2)}) collective-permute-start(f32[1,128,128]{2,1,0:T(8,128)S(1)} %collective-permute-done.15), channel_id=1, source_target_pairs={{0,16},{16,32},{32,48},{48,64},{64,80},{80,96},{96,112},{112,128},... | collective-permute-start | bytes 196616 | tf_op jit(solution)/shard_map/ppermute | solution.py:18
  154.0 4.9 %collective-permute-start.18 = (f32[1,128,128]{2,1,0:T(8,128)S(1)}, f32[1,128,128]{2,1,0:T(8,128)S(1)}, u32[]{:S(2)}, u32[]{:S(2)}) collective-permute-start(f32[1,128,128]{2,1,0:T(8,128)S(1)} %collective-permute-done.16), channel_id=1, source_target_pairs={{0,240},{16,0},{32,16},{48,32},{64,48},{80,64},{96,80},{112,96},{1... | collective-permute-start | bytes 196616 | tf_op jit(solution)/shard_map/ppermute | solution.py:23
  158.9 4.9 %collective-permute-start.19 = (f32[1,128,128]{2,1,0:T(8,128)S(1)}, f32[1,128,128]{2,1,0:T(8,128)S(1)}, u32[]{:S(2)}, u32[]{:S(2)}) collective-permute-start(f32[1,128,128]{2,1,0:T(8,128)S(1)} %collective-permute-done.17), channel_id=1, source_target_pairs={{0,16},{16,32},{32,48},{48,64},{64,80},{80,96},{96,112},{112,128},... | collective-permute-start | bytes 196616 | tf_op jit(solution)/shard_map/ppermute | solution.py:18
  159.0 4.9 %copy-start = (f32[16,128,128]{2,1,0:T(8,128)}, f32[16,128,128]{2,1,0:T(8,128)S(1)}, u32[]{:S(2)}) copy-start(f32[16,128,128]{2,1,0:T(8,128)S(1)} %constant_dynamic-update-slice_fusion.1) | copy-start | bytes 3145732
